TPU v7x, 32 devices: a whole 2x2x4 slice. The times are simulated.
32 devices in a mesh: dp: 4 (over y, x), expert: 8 (over z, core).
Axes of the slice: x: 2, y: 2, z: 4, core: 2. Of those that a mesh axis runs over, the one named last changes fastest.
Arguments:
- inputs: bfloat16 [32768, 768], P(('dp', 'expert')), may hold values from -6 to 6
- cotangent: bfloat16 [32768, 768], P(('dp', 'expert')), may hold values from -6 to 6
- seq_group: int32 [32], P(('dp', 'expert')), may hold values from 0 to 7
- domain_counts: int32 [8], replicated, may hold values from 1 to 8
- sort_order: int32 [32, 1024], P(('dp', 'expert')), may hold values from 0 to 1023, each once within a row
- send_counts: int32 [32, 8], P(('dp', 'expert')), may hold values from 0 to 256, as said below
- gain_one: float32 [768], replicated, may hold values from 0.5 to 1.5
- shift_one: float32 [768], replicated, may hold values from -1.2 to 1.2
- gain_two: float32 [768], replicated, may hold values from 0.5 to 1.5
- shift_two: float32 [768], replicated, may hold values from -1.2 to 1.2
- w_query: bfloat16 [768, 768], replicated, may hold values from -0.3125 to 0.3125
- w_key: bfloat16 [768, 768], replicated, may hold values from -0.3125 to 0.3125
- w_value: bfloat16 [768, 768], replicated, may hold values from -0.21875 to 0.21875
- w_out: bfloat16 [768, 768], replicated, may hold values from -0.875 to 0.875
- router: bfloat16 [768, 8], replicated, may hold values from -0.15625 to 0.15625
- expert_in: bfloat16 [8, 768, 3072], P('expert'), may hold values from -0.21875 to 0.21875
- expert_out: bfloat16 [8, 3072, 768], P('expert'), may hold values from -0.3125 to 0.3125
Outputs:
- output: bfloat16 [32768, 768], P(('dp', 'expert'))
- grad_inputs: bfloat16 [32768, 768], P(('dp', 'expert'))
- grad_gain_one: float32 [768], replicated
- grad_shift_one: float32 [768], replicated
- grad_gain_two: float32 [768], replicated
- grad_shift_two: float32 [768], replicated
- grad_w_query: float32 [768, 768], replicated
- grad_w_key: float32 [768, 768], replicated
- grad_w_value: float32 [768, 768], replicated
- grad_w_out: float32 [768, 768], replicated
- grad_expert_in: float32 [8, 768, 3072], P('expert')
- grad_expert_out: float32 [8, 3072, 768], P('expert')
Inputs may be any that keep to these rules, and one draw needn't show every extreme that they name: `send_counts`: each row sums to 1024. One expert, the same in every row, gets exactly 256 tokens from every device; in each row one other expert gets none and the rest get between 64 and 192. `sort_order`: each row is a permutation of the local token indices.
All inputs are finite; a program needn't handle non-finite values.
Results may differ from a plain program's by a relative error of at most 0.015.
The roundings to bfloat16 on the way count: a program that leaves them out, or rounds other values in their place, can miss the bound.
Values may be sent and summed in bfloat16 or wider, within the bound.
A program may use at most 256 MiB of HBM per device.

v0:
```python
import jax
import jax.numpy as jnp
from jax import lax
from jax.sharding import PartitionSpec as P

HEADS = 12
HEAD_DIM = 64
LEN = 1024
epsilon = 1e-05


def layer_norm(values_in, scales, offsets):
    center = values_in - jnp.mean(values_in, axis=-1, keepdims=True)
    spread = jnp.mean(center * center, axis=-1, keepdims=True)
    return center * lax.rsqrt(spread + epsilon) * scales + offsets


def exact_gelu(pre_act):
    return jax.nn.gelu(pre_act, approximate=False)


def local(
    inputs,
    cotangent,
    seq_group,
    domain_counts,
    sort_order,
    send_counts,
    gain_one,
    shift_one,
    gain_two,
    shift_two,
    w_query,
    w_key,
    w_value,
    w_out,
    router,
    expert_in,
    expert_out,
):
    tok_rows, model_width = inputs.shape
    seq_count = tok_rows // LEN
    experts_total = send_counts.shape[1]
    capacity = 2 * tok_rows // experts_total
    senders = lax.axis_size("expert")
    scale_factor = HEAD_DIM ** (-0.5)
    counts_row = send_counts[0]
    count_ends = jnp.cumsum(counts_row)
    count_starts = count_ends - counts_row
    places = jnp.arange(tok_rows, dtype=jnp.int32)
    expert_ids = jnp.arange(experts_total, dtype=jnp.int32)
    expert_at = jnp.sum((places[:, None] >= count_ends[None, :]).astype(jnp.int32), axis=1)
    slot_at = places - jnp.sum(
        jnp.where(expert_at[:, None] == expert_ids[None, :], count_starts[None, :], 0), axis=1
    )
    dest_token = (
        jnp.zeros((tok_rows,), jnp.int32).at[sort_order[0]].set(expert_at * capacity + slot_at)
    )
    expert_token = jnp.zeros((tok_rows,), jnp.int32).at[sort_order[0]].set(expert_at)
    choose = (expert_token[:, None] == expert_ids[None, :]).astype(jnp.bfloat16)
    router_rows = jnp.einsum("te,de->td", choose, router, preferred_element_type=jnp.float32)
    inputs_f = inputs.astype(jnp.float32)
    normed_b = layer_norm(inputs_f, gain_one, shift_one).astype(jnp.bfloat16)
    query_rows = jnp.dot(normed_b, w_query, preferred_element_type=jnp.float32).astype(jnp.bfloat16)
    key_rows = jnp.dot(normed_b, w_key, preferred_element_type=jnp.float32).astype(jnp.bfloat16)
    value_rows = jnp.dot(normed_b, w_value, preferred_element_type=jnp.float32).astype(jnp.bfloat16)

    def heads_first(matrix):
        return matrix.reshape(seq_count, LEN, HEADS, HEAD_DIM).transpose(2, 0, 1, 3)

    def tokens_first(matrix):
        return matrix.transpose(1, 2, 0, 3).reshape(tok_rows, HEADS * HEAD_DIM)

    positions = jnp.arange(LEN, dtype=jnp.int32)
    causal = positions[:, None] >= positions[None, :]

    def head_scores(query_h, key_h):
        scores = (
            jnp.einsum("sqd,skd->sqk", query_h, key_h, preferred_element_type=jnp.float32)
            * scale_factor
        )
        return jnp.where(causal[None], scores, -1000000000.0)

    def head_forward(pieces):
        query_h, key_h, value_h = pieces
        scores = head_scores(query_h, key_h)
        row_peak = jnp.max(scores, axis=-1, keepdims=True)
        exp_scores = jnp.exp(scores - row_peak)
        row_total = jnp.sum(exp_scores, axis=-1, keepdims=True)
        attention = (exp_scores / row_total).astype(jnp.bfloat16)
        head_out = jnp.einsum(
            "sqk,skd->sqd", attention, value_h, preferred_element_type=jnp.float32
        )
        return (head_out.astype(jnp.bfloat16), (row_peak + jnp.log(row_total))[..., 0])

    query_heads = heads_first(query_rows)
    key_heads = heads_first(key_rows)
    value_heads = heads_first(value_rows)
    mixed_heads, log_totals = lax.map(head_forward, (query_heads, key_heads, value_heads))
    mixed_rows = tokens_first(mixed_heads)
    branch = jnp.dot(mixed_rows, w_out, preferred_element_type=jnp.float32)
    hidden = inputs_f + branch
    routed = layer_norm(hidden, gain_two, shift_two)
    routed_b = routed.astype(jnp.bfloat16)
    gate_vals = jax.nn.sigmoid(jnp.sum(routed * router_rows, axis=1))
    send_rows = (
        jnp.zeros((experts_total * capacity, model_width), jnp.bfloat16)
        .at[dest_token]
        .set(routed_b)
    )
    arrived = lax.all_to_all(
        send_rows.reshape(experts_total, capacity, model_width),
        "expert",
        split_axis=0,
        concat_axis=0,
        tiled=True,
    ).reshape(senders * capacity, model_width)
    first_weight = expert_in[0]
    second_weight = expert_out[0]
    pre_act = jnp.dot(arrived, first_weight, preferred_element_type=jnp.float32)
    act_rows = exact_gelu(pre_act).astype(jnp.bfloat16)
    expert_rows = jnp.dot(act_rows, second_weight, preferred_element_type=jnp.float32).astype(
        jnp.bfloat16
    )
    returned = lax.all_to_all(
        expert_rows.reshape(senders, capacity, model_width),
        "expert",
        split_axis=0,
        concat_axis=0,
        tiled=True,
    ).reshape(experts_total * capacity, model_width)
    back_rows = returned[dest_token].astype(jnp.float32)
    output = (hidden + gate_vals[:, None] * back_rows).astype(jnp.bfloat16)
    inverse = 1.0 / domain_counts.astype(jnp.float32)
    domain_weights = inverse / jnp.mean(inverse)
    domain_ids = jnp.arange(domain_counts.shape[0], dtype=jnp.int32)
    seq_weight = jnp.sum(
        jnp.where(seq_group[:, None] == domain_ids[None, :], domain_weights[None, :], 0.0), axis=1
    )
    grad_output = (
        cotangent.astype(jnp.float32).reshape(seq_count, LEN, model_width)
        * seq_weight[:, None, None]
    ).reshape(tok_rows, model_width)
    grad_back = (gate_vals[:, None] * grad_output).astype(jnp.bfloat16)
    grad_logit = jnp.sum(back_rows * grad_output, axis=1) * gate_vals * (1.0 - gate_vals)
    send_grads = (
        jnp.zeros((experts_total * capacity, model_width), jnp.bfloat16)
        .at[dest_token]
        .set(grad_back)
    )
    grad_arrived = lax.all_to_all(
        send_grads.reshape(experts_total, capacity, model_width),
        "expert",
        split_axis=0,
        concat_axis=0,
        tiled=True,
    ).reshape(senders * capacity, model_width)
    grad_act = jnp.einsum(
        "rd,fd->rf", grad_arrived, second_weight, preferred_element_type=jnp.float32
    )
    gelu_back = jax.vjp(exact_gelu, pre_act)[1]
    grad_pre = gelu_back(grad_act)[0].astype(jnp.bfloat16)
    grad_second = jnp.einsum(
        "rf,rd->fd", act_rows, grad_arrived, preferred_element_type=jnp.float32
    )
    grad_first = jnp.einsum("rd,rf->df", arrived, grad_pre, preferred_element_type=jnp.float32)
    grad_sent = jnp.einsum(
        "rf,df->rd", grad_pre, first_weight, preferred_element_type=jnp.float32
    ).astype(jnp.bfloat16)
    grad_returned = lax.all_to_all(
        grad_sent.reshape(senders, capacity, model_width),
        "expert",
        split_axis=0,
        concat_axis=0,
        tiled=True,
    ).reshape(experts_total * capacity, model_width)
    grad_routed = grad_returned[dest_token].astype(jnp.float32) + grad_logit[:, None] * router_rows
    norm_back_two = jax.vjp(layer_norm, hidden, gain_two, shift_two)[1]
    grad_hidden_norm, grad_gain_two, grad_shift_two = norm_back_two(grad_routed)
    grad_hidden = grad_output + grad_hidden_norm
    grad_branch = grad_hidden.astype(jnp.bfloat16)
    grad_w_out = jnp.einsum(
        "td,te->de", mixed_rows, grad_branch, preferred_element_type=jnp.float32
    )
    grad_mixed = jnp.einsum(
        "te,de->td", grad_branch, w_out, preferred_element_type=jnp.float32
    ).astype(jnp.bfloat16)

    def head_backward(pieces):
        query_h, key_h, value_h, grad_h, log_total = pieces
        attention = jnp.exp(head_scores(query_h, key_h) - log_total[..., None])
        attention_b = attention.astype(jnp.bfloat16)
        grad_value = jnp.einsum(
            "sqk,sqd->skd", attention_b, grad_h, preferred_element_type=jnp.float32
        )
        grad_attention = jnp.einsum(
            "sqd,skd->sqk", grad_h, value_h, preferred_element_type=jnp.float32
        )
        row_delta = jnp.sum(attention * grad_attention, axis=-1, keepdims=True)
        grad_scores = (attention * (grad_attention - row_delta)).astype(jnp.bfloat16)
        grad_query = (
            jnp.einsum("sqk,skd->sqd", grad_scores, key_h, preferred_element_type=jnp.float32)
            * scale_factor
        )
        grad_key = (
            jnp.einsum("sqk,sqd->skd", grad_scores, query_h, preferred_element_type=jnp.float32)
            * scale_factor
        )
        return (
            grad_query.astype(jnp.bfloat16),
            grad_key.astype(jnp.bfloat16),
            grad_value.astype(jnp.bfloat16),
        )

    grad_q_heads, grad_k_heads, grad_v_heads = lax.map(
        head_backward, (query_heads, key_heads, value_heads, heads_first(grad_mixed), log_totals)
    )
    grad_queries = tokens_first(grad_q_heads)
    grad_keys = tokens_first(grad_k_heads)
    grad_values = tokens_first(grad_v_heads)
    grad_w_query = jnp.einsum(
        "td,te->de", normed_b, grad_queries, preferred_element_type=jnp.float32
    )
    grad_w_key = jnp.einsum("td,te->de", normed_b, grad_keys, preferred_element_type=jnp.float32)
    grad_w_value = jnp.einsum(
        "td,te->de", normed_b, grad_values, preferred_element_type=jnp.float32
    )
    grad_normed = jnp.einsum("te,de->td", grad_queries, w_query, preferred_element_type=jnp.float32)
    grad_normed = grad_normed + jnp.einsum(
        "te,de->td", grad_keys, w_key, preferred_element_type=jnp.float32
    )
    grad_normed = grad_normed + jnp.einsum(
        "te,de->td", grad_values, w_value, preferred_element_type=jnp.float32
    )
    norm_back_one = jax.vjp(layer_norm, inputs_f, gain_one, shift_one)[1]
    grad_input_norm, grad_gain_one, grad_shift_one = norm_back_one(grad_normed)
    grad_inputs = (grad_hidden + grad_input_norm).astype(jnp.bfloat16)
    expert_sums = (
        lax.psum(grad_first.astype(jnp.bfloat16), "dp").astype(jnp.float32),
        lax.psum(grad_second.astype(jnp.bfloat16), "dp").astype(jnp.float32),
    )
    dense_sums = lax.psum(
        (
            grad_w_query,
            grad_w_key,
            grad_w_value,
            grad_w_out,
            grad_gain_one,
            grad_shift_one,
            grad_gain_two,
            grad_shift_two,
        ),
        ("dp", "expert"),
    )
    return (
        output,
        grad_inputs,
        dense_sums[4],
        dense_sums[5],
        dense_sums[6],
        dense_sums[7],
        dense_sums[0],
        dense_sums[1],
        dense_sums[2],
        dense_sums[3],
        expert_sums[0][None],
        expert_sums[1][None],
    )


def solution(mesh):
    return jax.shard_map(
        local,
        mesh=mesh,
        in_specs=(
            P(("dp", "expert"), None),
            P(("dp", "expert"), None),
            P(("dp", "expert")),
            P(),
            P(("dp", "expert"), None),
            P(("dp", "expert"), None),
            P(),
            P(),
            P(),
            P(),
            P(),
            P(),
            P(),
            P(),
            P(),
            P("expert", None, None),
            P("expert", None, None),
        ),
        out_specs=(
            P(("dp", "expert"), None),
            P(("dp", "expert"), None),
            P(),
            P(),
            P(),
            P(),
            P(),
            P(),
            P(),
            P(),
            P("expert", None, None),
            P("expert", None, None),
        ),
        check_vma=False,
    )
```

profile of v0, /device:TPU:0, one launch (start us, length us, event | category | flops | bytes accessed | tf_op | source)
XLA Modules:
  0.0 991.7 jit_solution(5724763379888539284)
XLA Ops:
  34.1 62.7 %while.28 = (s32[]{:T(128)}, bf16[12,1,1024,64]{2,3,1,0:T(8,128)(2,1)}, f32[12,1,1024]{2,1,0:T(1,128)}, bf16[12,1,1024,64]{3,2,1,0:T(8,128)(2,1)}, bf16[12,1,102...) while((s32[]{:T(128)}, bf16[12,1,1024,64]{2,3,1,0:T(8,128)(2,1)}, ...), condition=%wide.region_5.6_spmd.clone, body=%wide.region_2.5_spmd.clone.sunk | while | flops 284228608 | bytes 13544013 | solution.py:99
  103.0 4.8 scatter_custom_fusion
  107.8 5.1 multiply_reduce_fusion.3
  119.6 7.9 scatter_custom_fusion.2
  127.5 78.0 %all_to_all.20 = bf16[8,256,768]{2,1,0:T(8,128)(2,1)S(1)} all-to-all(bf16[8,256,768]{2,1,0:T(8,128)(2,1)} %bitcast.180), channel_id=1, replica_groups=mesh['dp'=4,'expert'=8] {'expert'}, dimensions={0} | all-to-all | bytes 6291456 | tf_op jit(solution)/shard_map/all_to_all | solution.py:111
  205.5 63.5 %multiply_convert_fusion.1 = (bf16[2048,3072]{1,0:T(8,128)(2,1)S(1)}, f32[2048,3072]{1,0:T(8,128)}, f32[2048,3072]{1,0:T(8,128)}) fusion(bf16[2048,768]{1,0:T(8,128)(2,1)S(1)} %bitcast.185, bf16[1,768,3072]{2,1,0:T(8,128)(2,1)} %param.36), kind=kOutput, calls=%fused_computation.72 | convolution fusion | flops 10072621056 | bytes 70778880 | tf_op jit(solution)/shard_map/dot_general | solution.py:120
  269.0 11.2 %fusion.82 = bf16[2048,768]{1,0:T(8,128)(2,1)} fusion(bf16[2048,3072]{1,0:T(8,128)(2,1)S(1)} %get-tuple-element.228, bf16[1,3072,768]{2,1,0:T(8,128)(2,1)S(1)} %copy-done.42), kind=kOutput, calls=%fused_computation.111 | convolution fusion | flops 9665249280 | bytes 20447232 | tf_op jit(solution)/shard_map/dot_general | solution.py:122
  280.2 4.7 all-to-all-start.1
  289.3 67.2 %all-to-all-done.1 = bf16[8,256,768]{2,1,0:T(8,128)(2,1)} async-done(((bf16[8,256,768]{2,1,0:T(8,128)(2,1)}), bf16[8,256,768]{2,1,0:T(8,128)(2,1)}, u32[]{:S(2)}, u32[]{:S(2)}) %all-to-all-start.1) | async-done | bytes 3145760 | tf_op jit(solution)/shard_map/all_to_all | solution.py:125
  356.5 7.9 gather_fusion
  373.4 7.9 scatter_custom_fusion.3
  381.3 76.2 %all_to_all.21 = bf16[8,256,768]{2,1,0:T(8,128)(2,1)} all-to-all(bf16[8,256,768]{2,1,0:T(8,128)(2,1)} %bitcast.179), channel_id=1, replica_groups=mesh['dp'=4,'expert'=8] {'expert'}, dimensions={0} | all-to-all | bytes 6291456 | tf_op jit(solution)/shard_map/all_to_all | solution.py:151
  457.6 32.8 %add_convert_fusion = bf16[2048,3072]{1,0:T(8,128)(2,1)} fusion(f32[2048,3072]{1,0:T(8,128)} %get-tuple-element.229, f32[2048,3072]{1,0:T(8,128)} %get-tuple-element.244, bf16[2048,768]{1,0:T(8,128)(2,1)} %bitcast.188, bf16[1,3072,768]{2,1,0:T(8,128)(2,1)} %param.37), kind=kOutput, calls=%fused_computation.71 | convolution fusion | flops 9751756800 | bytes 70778880 | tf_op jit(solution)/shard_map/rd,fd->rf/dot_general | solution.py:158
  490.4 15.4 %fusion.79 = bf16[2048,768]{1,0:T(8,128)(2,1)} fusion(bf16[2048,3072]{1,0:T(8,128)(2,1)} %add_convert_fusion, bf16[1,768,3072]{2,1,0:T(8,128)(2,1)} %param.36), kind=kOutput, calls=%fused_computation.110 | convolution fusion | flops 9665249280 | bytes 20447232 | tf_op jit(solution)/shard_map/rf,df->rd/dot_general | solution.py:167
  510.8 15.5 %fusion.76 = bf16[1,3072,768]{2,1,0:T(8,128)(2,1)} fusion(bf16[2048,3072]{1,0:T(8,128)(2,1)} %copy-done.49, bf16[2048,768]{1,0:T(8,128)(2,1)} %bitcast.189), kind=kOutput, calls=%fused_computation.105 | convolution fusion | flops 9666035712 | bytes 20447232 | tf_op jit(solution)/shard_map/rf,rd->fd/dot_general | solution.py:163
  526.4 14.5 %fusion.75 = bf16[1,768,3072]{2,1,0:T(8,128)(2,1)} fusion(bf16[2048,768]{1,0:T(8,128)(2,1)S(1)} %bitcast.186, bf16[2048,3072]{1,0:T(8,128)(2,1)} %add_convert_fusion), kind=kOutput, calls=%fused_computation.104 | convolution fusion | flops 9666035712 | bytes 20447232 | tf_op jit(solution)/shard_map/rd,rf->df/dot_general | solution.py:166
  541.1 40.7 %all-to-all-done.3 = bf16[8,256,768]{2,1,0:T(8,128)(2,1)} async-done(((bf16[8,256,768]{2,1,0:T(8,128)(2,1)}), bf16[8,256,768]{2,1,0:T(8,128)(2,1)}, u32[]{:S(2)}, u32[]{:S(2)}) %all-to-all-start.3) | async-done | bytes 3145760 | tf_op jit(solution)/shard_map/all_to_all | solution.py:170
  581.8 7.9 gather_fusion.1
  592.4 4.9 multiply_reduce_fusion.1
  612.5 151.5 %while.29 = (s32[]{:T(128)}, bf16[12,1,1024,64]{2,3,1,0:T(8,128)(2,1)}, bf16[12,1,1024,64]{2,3,1,0:T(8,128)(2,1)}, bf16[12,1,1024,64]{2,3,1,0:T(8,128)(2,1)}, bf...) while((s32[]{:T(128)}, ...), condition=%wide.region_23.24_spmd.clone, body=%wide.region_21.23_spmd.clone.sunk | while | flops 681901056 | bytes 33711208 | solution.py:215
  764.1 4.8 fusion.124
  802.1 40.3 %all-reduce = (f32[768]{0:T(1024)}, f32[768]{0:T(1024)}, f32[768]{0:T(1024)}, f32[768]{0:T(1024)}) all-reduce(f32[768]{0:T(1024)S(1)} %get-tuple-element.181, f32[768]{0:T(1024)S(1)} %get-tuple-element.184, f32[768]{0:T(1024)S(1)} %get-tuple-element.179, ...), channel_id=1, replica_groups=mesh['dp'=4,'expert'=8] {'dp','expert'}, use_global_device_ids=true, to_apply=%region_27.28 | all-reduce | flops 3072 | bytes 24576 | tf_op jit(solution)/shard_map/psum | solution.py:242
  842.4 7.5 broadcast_in_dim.122
  854.4 120.3 %all-reduce.6.cloned.1.call-done = (f32[768,768]{1,0:T(8,128)}, f32[768,768]{1,0:T(8,128)}, f32[768,768]{1,0:T(8,128)}, f32[768,768]{1,0:T(8,128)}) async-done(((f32[768,768]{1,0:T(8,128)}, f32[768,768]{1,0:T(8,128)}, f32[768,768]{1,0:T(8,128)}, f32[768,768]{1,0:T(8,128)}), (f32[768,768]{1,0:T(8,128)}, f32[768,768]{1,0:T(8,128)}, f32[768,768]{1,0:T(8,128)}, ...) | async-done | bytes 9437200 | tf_op jit(solution)/shard_map/psum | solution.py:242
  (311 shorter events, 335.7 us)
Async XLA Ops:
  7.2 10.6 %copy-start = (bf16[768,768]{1,0:T(8,128)(2,1)S(1)}, bf16[768,768]{1,0:T(8,128)(2,1)}, u32[]{:S(2)}) copy-start(bf16[768,768]{1,0:T(8,128)(2,1)} %param.33) | copy-start | bytes 3538948
  9.0 87.7 %copy-start.1 = (bf16[1024,768]{0,1:T(8,128)(2,1)}, bf16[1024,768]{0,1:T(8,128)(2,1)S(1)}, u32[]{:S(2)}) copy-start(bf16[1024,768]{0,1:T(8,128)(2,1)S(1)} %copy.57) | copy-start | bytes 4718596
  9.3 15.3 %copy-start.21 = (f32[1024]{0:T(1024)}, f32[1024]{0:T(1024)S(1)}, u32[]{:S(2)}) copy-start(f32[1024]{0:T(1024)S(1)} %broadcast_multiply_fusion.1) | copy-start | bytes 12292
  10.9 13.7 %copy-start.30 = (f32[1024]{0:T(1024)}, f32[1024]{0:T(1024)S(1)}, u32[]{:S(2)}) copy-start(f32[1024]{0:T(1024)S(1)} %fusion.102) | copy-start | bytes 12292
  100.0 7.8 copy-start.25
  100.1 7.8 copy-start.37
  100.1 7.8 copy-start.38
  100.1 12.9 %copy-start.19 = (f32[1024]{0:T(1024)}, f32[1024]{0:T(1024)S(1)}, u32[]{:S(2)}) copy-start(f32[1024]{0:T(1024)S(1)} %broadcast_multiply_fusion) | copy-start | bytes 12292
  102.7 10.3 %copy-start.23 = (f32[1024]{0:T(1024)}, f32[1024]{0:T(1024)S(1)}, u32[]{:S(2)}) copy-start(f32[1024]{0:T(1024)S(1)} %fusion.103) | copy-start | bytes 12292
  119.6 85.9 %copy-start.39 = (s32[1024]{0:T(1024)}, s32[1024]{0:T(1024)S(1)}, u32[]{:S(2)}) copy-start(s32[1024]{0:T(1024)S(1)} %get-tuple-element.240) | copy-start | bytes 12292
  205.5 63.5 %copy-start.13 = (bf16[8,256,768]{2,1,0:T(8,128)(2,1)}, bf16[8,256,768]{2,1,0:T(8,128)(2,1)S(1)}, u32[]{:S(2)}) copy-start(bf16[8,256,768]{2,1,0:T(8,128)(2,1)S(1)} %all_to_all.20) | copy-start | bytes 9437188
  205.5 63.5 %copy-start.42 = (bf16[1,3072,768]{2,1,0:T(8,128)(2,1)S(1)}, bf16[1,3072,768]{2,1,0:T(8,128)(2,1)}, u32[]{:S(2)}) copy-start(bf16[1,3072,768]{2,1,0:T(8,128)(2,1)} %param.37) | copy-start | bytes 14155780
  269.0 11.3 %copy-start.49 = (bf16[2048,3072]{1,0:T(8,128)(2,1)}, bf16[2048,3072]{1,0:T(8,128)(2,1)S(1)}, u32[]{:S(2)}) copy-start(bf16[2048,3072]{1,0:T(8,128)(2,1)S(1)} %get-tuple-element.228) | copy-start | bytes 37748740
  280.2 76.2 %all-to-all-start.1 = ((bf16[8,256,768]{2,1,0:T(8,128)(2,1)}), bf16[8,256,768]{2,1,0:T(8,128)(2,1)}, u32[]{:S(2)}, u32[]{:S(2)}) async-start(bf16[8,256,768]{2,1,0:T(8,128)(2,1)} %bitcast.190), calls=%async_computation.1 | async-start | bytes 6291456 | tf_op jit(solution)/shard_map/all_to_all | solution.py:125
  285.0 71.5 %copy-start.36 = (s32[1024]{0:T(1024)S(1)}, s32[1024]{0:T(1024)}, u32[]{:S(2)}) copy-start(s32[1024]{0:T(1024)} %get-tuple-element.239) | copy-start | bytes 12292
  286.7 315.3 %copy-start.8 = (bf16[1024,768]{0,1:T(8,128)(2,1)}, bf16[1024,768]{0,1:T(8,128)(2,1)S(1)}, u32[]{:S(2)}) copy-start(bf16[1024,768]{0,1:T(8,128)(2,1)S(1)} %copy.63) | copy-start | bytes 4718596
  505.8 76.0 %all-to-all-start.3 = ((bf16[8,256,768]{2,1,0:T(8,128)(2,1)}), bf16[8,256,768]{2,1,0:T(8,128)(2,1)}, u32[]{:S(2)}, u32[]{:S(2)}) async-start(bf16[8,256,768]{2,1,0:T(8,128)(2,1)} %bitcast.187), calls=%async_computation.3 | async-start | bytes 6291456 | tf_op jit(solution)/shard_map/all_to_all | solution.py:170
  510.3 332.1 %all-reduce.8.cloned.1.call-start = ((), (), s32[]{:S(2)}) async-start(), calls=%async_computation.5 | async-start | bytes 18874368 | tf_op jit(solution)/shard_map/psum | solution.py:239
  510.8 15.6 %copy-start.14 = (bf16[8,256,768]{2,1,0:T(8,128)(2,1)S(1)}, bf16[8,256,768]{2,1,0:T(8,128)(2,1)}, u32[]{:S(2)}) copy-start(bf16[8,256,768]{2,1,0:T(8,128)(2,1)} %copy-done.13) | copy-start | bytes 9437188
  540.9 433.8 %all-reduce.6.cloned.1.call-start = ((), (), s32[]{:S(2)}) async-start(), calls=%async_computation.4 | async-start | bytes 18874368 | tf_op jit(solution)/shard_map/psum | solution.py:242
  592.3 5.0 copy-start.4
  592.3 5.3 copy-start.5
  592.4 5.7 copy-start.10
  842.4 7.5 copy-start.12
  (30 other events, 88.2 us)
Sparse Core Ops, SparseCore 0:
  541.0 190.5 all-reduce.7
  782.4 192.1 all-reduce.5
where the time goes:
time: 1000 us; the launch traced here: 992 us
  matrix products  378 us (38%)
  waiting for transfers between devices  228 us (23%)
  blocking collectives  195 us (20%)
  local copies, waits for them, and re-layouts  110 us (11%)
  other arithmetic  54.5 us (5%)
  between operations  16.4 us (2%)
    psum x1, waiting for transfers between devices, local(): lax.psum((grad_w_query, grad_w_key, grad_w_value, grad_w_out, grad_gain_o...  120 us
    all_to_all x1, blocking collectives, local(): lax.all_to_all(send_rows.reshape(experts_total, capacity, model_width), '...  78 us
    all_to_all x1, blocking collectives, local(): lax.all_to_all(send_grads.reshape(experts_total, capacity, model_width),...  76.2 us
    all_to_all x1, waiting for transfers between devices, local(): lax.all_to_all(expert_rows.reshape(senders, capacity, model_width), 'expe...  67.2 us
    dot_general x1, matrix products, local(): pre_act = jnp.dot(arrived, first_weight, preferred_element_type=jnp.float32)  63.5 us
    dot_general x24, matrix products, head_scores(): jnp.einsum('sqd,skd->sqk', query_h, key_h, preferred_element_type=jnp.flo...  46.3 us
    all_to_all x1, waiting for transfers between devices, local(): lax.all_to_all(grad_sent.reshape(senders, capacity, model_width), 'expert...  40.7 us
    psum x1, blocking collectives, local(): lax.psum((grad_w_query, grad_w_key, grad_w_value, grad_w_out, grad_gain_o...  40.3 us
  transfers between devices with their start and end apart: 4, of which 3 were waited for; matrix products, arithmetic and copies ran while one was open for 26% of the time, Pallas kernels for 0%

commit v1 on v0

--- a/solution.py
+++ b/solution.py
@@ -240,17 +240,20 @@
         lax.psum(grad_second.astype(jnp.bfloat16), "dp").astype(jnp.float32),
     )
     dense_sums = lax.psum(
-        (
-            grad_w_query,
-            grad_w_key,
-            grad_w_value,
-            grad_w_out,
-            grad_gain_one,
-            grad_shift_one,
-            grad_gain_two,
-            grad_shift_two,
+        lax.psum(
+            (
+                grad_w_query,
+                grad_w_key,
+                grad_w_value,
+                grad_w_out,
+                grad_gain_one,
+                grad_shift_one,
+                grad_gain_two,
+                grad_shift_two,
+            ),
+            "expert",
         ),
-        ("dp", "expert"),
+        "dp",
     )
     return (
         output,

time: 1000 us -> 1390 us (1.39)
  waiting for transfers between devices: 228 us -> 616 us
    psum x0 -> x1, waiting for transfers between devices: none -> 182 us  [local(): lax.psum(lax.psum((grad_w_query, grad_w_key, grad_w_value, grad_w_out, gr...]
    psum x1, waiting for transfers between devices: 0.01 us -> 131 us  [local(): lax.psum(grad_first.astype(jnp.bfloat16), 'dp').astype(jnp.float32)]
    psum x1, waiting for transfers between devices: 120 us -> 165 us  [local(): lax.psum((grad_w_query, grad_w_key, grad_w_value, grad_w_out, grad_gain_o...]
    all_to_all x1, waiting for transfers between devices: 40.7 us -> 71 us  [local(): lax.all_to_all(grad_sent.reshape(senders, capacity, model_width), 'expert...]
    psum x0 -> x1, blocking collectives: none -> 17 us  [local(): lax.psum(lax.psum((grad_w_query, grad_w_key, grad_w_value, grad_w_out, gr...]
  transfers between devices with their start and end apart: 4 -> 5, of which waited for: 3 -> 5; matrix products, arithmetic and copies ran while one was open for 26% -> 5% of each run, Pallas kernels for 0% -> 0%
where the time goes in v1:
time: 1390 us; the launch traced here: 1380 us
  waiting for transfers between devices  616 us (44%)
  matrix products  373 us (27%)
  blocking collectives  198 us (14%)
  local copies, waits for them, and re-layouts  109 us (8%)
  other arithmetic  54.5 us (4%)
  between operations  15.9 us (1%)
    psum x1, waiting for transfers between devices, local(): lax.psum(lax.psum((grad_w_query, grad_w_key, grad_w_value, grad_w_out, gr...  182 us
    psum x1, waiting for transfers between devices, local(): lax.psum((grad_w_query, grad_w_key, grad_w_value, grad_w_out, grad_gain_o...  165 us
    psum x1, waiting for transfers between devices, local(): lax.psum(grad_first.astype(jnp.bfloat16), 'dp').astype(jnp.float32)  131 us
    all_to_all x1, blocking collectives, local(): lax.all_to_all(send_rows.reshape(experts_total, capacity, model_width), '...  78 us
    all_to_all x1, blocking collectives, local(): lax.all_to_all(send_grads.reshape(experts_total, capacity, model_width),...  76.2 us
    all_to_all x1, waiting for transfers between devices, local(): lax.all_to_all(grad_sent.reshape(senders, capacity, model_width), 'expert...  71 us
    all_to_all x1, waiting for transfers between devices, local(): lax.all_to_all(expert_rows.reshape(senders, capacity, model_width), 'expe...  67.2 us
    dot_general x1, matrix products, local(): pre_act = jnp.dot(arrived, first_weight, preferred_element_type=jnp.float32)  63.5 us
  transfers between devices with their start and end apart: 5, of which 5 were waited for; matrix products, arithmetic and copies ran while one was open for 5% of the time, Pallas kernels for 0%

profile of v1, /device:TPU:0, one launch (start us, length us, event | category | flops | bytes accessed | tf_op | source)
XLA Modules:
  0.0 1377.5 jit_solution(715133831639086327)
XLA Ops:
  34.1 62.7 %while.28 = (s32[]{:T(128)}, bf16[12,1,1024,64]{2,3,1,0:T(8,128)(2,1)}, f32[12,1,1024]{2,1,0:T(1,128)}, bf16[12,1,1024,64]{3,2,1,0:T(8,128)(2,1)}, bf16[12,1,102...) while((s32[]{:T(128)}, bf16[12,1,1024,64]{2,3,1,0:T(8,128)(2,1)}, ...), condition=%wide.region_5.6_spmd.clone, body=%wide.region_2.5_spmd.clone.sunk | while | flops 284228608 | bytes 13544013 | solution.py:99
  107.5 5.1 multiply_reduce_fusion.3
  119.2 8.0 scatter_custom_fusion.2
  127.2 78.0 %all_to_all.20 = bf16[8,256,768]{2,1,0:T(8,128)(2,1)S(1)} all-to-all(bf16[8,256,768]{2,1,0:T(8,128)(2,1)} %bitcast.180), channel_id=1, replica_groups=mesh['dp'=4,'expert'=8] {'expert'}, dimensions={0} | all-to-all | bytes 6291456 | tf_op jit(solution)/shard_map/all_to_all | solution.py:111
  205.2 63.5 %multiply_convert_fusion.1 = (bf16[2048,3072]{1,0:T(8,128)(2,1)S(1)}, f32[2048,3072]{1,0:T(8,128)}, f32[2048,3072]{1,0:T(8,128)}) fusion(bf16[2048,768]{1,0:T(8,128)(2,1)S(1)} %bitcast.185, bf16[1,768,3072]{2,1,0:T(8,128)(2,1)} %param.36), kind=kOutput, calls=%fused_computation.72 | convolution fusion | flops 10072621056 | bytes 70778880 | tf_op jit(solution)/shard_map/dot_general | solution.py:120
  268.7 11.3 fusion.82
  289.0 67.2 %all-to-all-done.1 = bf16[8,256,768]{2,1,0:T(8,128)(2,1)} async-done(((bf16[8,256,768]{2,1,0:T(8,128)(2,1)}), bf16[8,256,768]{2,1,0:T(8,128)(2,1)}, u32[]{:S(2)}, u32[]{:S(2)}) %all-to-all-start.1) | async-done | bytes 3145760 | tf_op jit(solution)/shard_map/all_to_all | solution.py:125
  356.2 7.9 gather_fusion
  373.2 7.9 scatter_custom_fusion.3
  381.0 76.2 %all_to_all.21 = bf16[8,256,768]{2,1,0:T(8,128)(2,1)} all-to-all(bf16[8,256,768]{2,1,0:T(8,128)(2,1)} %bitcast.179), channel_id=1, replica_groups=mesh['dp'=4,'expert'=8] {'expert'}, dimensions={0} | all-to-all | bytes 6291456 | tf_op jit(solution)/shard_map/all_to_all | solution.py:151
  457.3 32.7 %add_convert_fusion = bf16[2048,3072]{1,0:T(8,128)(2,1)} fusion(f32[2048,3072]{1,0:T(8,128)} %get-tuple-element.237, f32[2048,3072]{1,0:T(8,128)} %get-tuple-element.252, bf16[2048,768]{1,0:T(8,128)(2,1)} %bitcast.187, bf16[1,3072,768]{2,1,0:T(8,128)(2,1)} %param.37), kind=kOutput, calls=%fused_computation.71 | convolution fusion | flops 9751756800 | bytes 70778880 | tf_op jit(solution)/shard_map/rd,fd->rf/dot_general | solution.py:158
  489.9 15.5 %fusion.79 = bf16[2048,768]{1,0:T(8,128)(2,1)} fusion(bf16[2048,3072]{1,0:T(8,128)(2,1)} %add_convert_fusion, bf16[1,768,3072]{2,1,0:T(8,128)(2,1)} %param.36), kind=kOutput, calls=%fused_computation.110 | convolution fusion | flops 9665249280 | bytes 20447232 | tf_op jit(solution)/shard_map/rf,df->rd/dot_general | solution.py:167
  510.4 71.0 %all-to-all-done.3 = bf16[8,256,768]{2,1,0:T(8,128)(2,1)} async-done(((bf16[8,256,768]{2,1,0:T(8,128)(2,1)}), bf16[8,256,768]{2,1,0:T(8,128)(2,1)}, u32[]{:S(2)}, u32[]{:S(2)}) %all-to-all-start.3) | async-done | bytes 3145760 | tf_op jit(solution)/shard_map/all_to_all | solution.py:170
  581.4 7.9 gather_fusion.1
  615.6 150.9 %while.29 = (s32[]{:T(128)}, bf16[12,1,1024,64]{2,3,1,0:T(8,128)(2,1)}, bf16[12,1,1024,64]{2,3,1,0:T(8,128)(2,1)}, bf16[12,1,1024,64]{2,3,1,0:T(8,128)(2,1)}, bf...) while((s32[]{:T(128)}, ...), condition=%wide.region_23.24_spmd.clone, body=%wide.region_21.23_spmd.clone.sunk | while | flops 681901056 | bytes 33711208 | solution.py:215
  777.3 15.5 %fusion.76 = bf16[1,3072,768]{2,1,0:T(8,128)(2,1)} fusion(bf16[2048,3072]{1,0:T(8,128)(2,1)} %copy-done.51, bf16[2048,768]{1,0:T(8,128)(2,1)} %bitcast.188), kind=kOutput, calls=%fused_computation.105 | convolution fusion | flops 9666035712 | bytes 20447232 | tf_op jit(solution)/shard_map/rf,rd->fd/dot_general | solution.py:163
  792.9 14.6 %fusion.75 = bf16[1,768,3072]{2,1,0:T(8,128)(2,1)} fusion(bf16[2048,768]{1,0:T(8,128)(2,1)S(1)} %bitcast.186, bf16[2048,3072]{1,0:T(8,128)(2,1)} %add_convert_fusion), kind=kOutput, calls=%fused_computation.104 | convolution fusion | flops 9666035712 | bytes 20447232 | tf_op jit(solution)/shard_map/rd,rf->df/dot_general | solution.py:166
  807.7 165.0 %all-reduce.9.cloned.1.call-done = (f32[768,768]{1,0:T(8,128)}, f32[768,768]{1,0:T(8,128)}, f32[768,768]{1,0:T(8,128)}, f32[768,768]{1,0:T(8,128)}) async-done(((f32[768,768]{1,0:T(8,128)}, f32[768,768]{1,0:T(8,128)}, f32[768,768]{1,0:T(8,128)}, f32[768,768]{1,0:T(8,128)}), (f32[768,768]{1,0:T(8,128)}, f32[768,768]{1,0:T(8,128)}, f32[768,768]{1,0:T(8,128)}, ...) | async-done | bytes 9437200 | tf_op jit(solution)/shard_map/psum | solution.py:243
  991.7 27.1 %all-reduce = (f32[768]{0:T(1024)S(1)}, f32[768]{0:T(1024)S(1)}, f32[768]{0:T(1024)S(1)}, f32[768]{0:T(1024)S(1)}) all-reduce(f32[768]{0:T(1024)S(1)} %get-tuple-element.181, f32[768]{0:T(1024)S(1)} %get-tuple-element.184, f32[768]{0:T(1024)S(1)} %get-tuple-element.179, ...), channel_id=1, replica_groups=mesh['dp'=4,'expert'=8] {'expert'}, use_global_device_ids=true, to_apply=%region_27.28 | all-reduce | flops 3072 | bytes 24576 | tf_op jit(solution)/shard_map/psum | solution.py:243
  1018.8 17.0 %all-reduce.2 = (f32[768]{0:T(1024)}, f32[768]{0:T(1024)}, f32[768]{0:T(1024)}, f32[768]{0:T(1024)}) all-reduce(f32[768]{0:T(1024)S(1)} %get-tuple-element.216, f32[768]{0:T(1024)S(1)} %get-tuple-element.217, f32[768]{0:T(1024)S(1)} %get-tuple-element.218, f32[768]{0:T(1024)S(1)} %get-tuple-element.219), channel_id=1, replica_groups=mesh['dp'=4,'expert'=8] {'dp'}, use_global_device_ids=true, to_apply=%region_28.29 | all-reduce | flops 3072 | bytes 24576 | tf_op jit(solution)/shard_map/psum | solution.py:242
  1035.8 130.9 %all-reduce.13.cloned.1.call-done = (bf16[1,768,3072]{2,1,0:T(8,128)(2,1)}, bf16[1,3072,768]{2,1,0:T(8,128)(2,1)}) async-done(((bf16[1,768,3072]{2,1,0:T(8,128)(2,1)}, bf16[1,3072,768]{2,1,0:T(8,128)(2,1)}), (bf16[1,768,3072]{2,1,0:T(8,128)(2,1)}, bf16[1,3072,768]{2,1,0:T(8,128)(2,1)})) %all-reduce.13.cloned.1.call-update) | async-done | bytes 9437200 | tf_op jit(solution)/shard_map/psum | solution.py:239
  1166.7 7.5 broadcast_in_dim.122
  1174.3 4.9 broadcast_in_dim.124
  1179.2 181.8 %all-reduce.11.cloned.1.call-done = (f32[768,768]{1,0:T(8,128)}, f32[768,768]{1,0:T(8,128)}, f32[768,768]{1,0:T(8,128)}, f32[768,768]{1,0:T(8,128)}) async-done(((f32[768,768]{1,0:T(8,128)}, f32[768,768]{1,0:T(8,128)}, f32[768,768]{1,0:T(8,128)}, f32[768,768]{1,0:T(8,128)}), (f32[768,768]{1,0:T(8,128)}, f32[768,768]{1,0:T(8,128)}, f32[768,768]{1,0:T(8,128)}, ...) | async-done | bytes 9437200 | tf_op jit(solution)/shard_map/psum | solution.py:242
  (319 shorter events, 344.7 us)
Async XLA Ops:
  7.2 10.6 copy-start
  9.0 87.7 %copy-start.1 = (bf16[1024,768]{0,1:T(8,128)(2,1)}, bf16[1024,768]{0,1:T(8,128)(2,1)S(1)}, u32[]{:S(2)}) copy-start(bf16[1024,768]{0,1:T(8,128)(2,1)S(1)} %copy.57) | copy-start | bytes 4718596
  9.3 15.3 %copy-start.23 = (f32[1024]{0:T(1024)}, f32[1024]{0:T(1024)S(1)}, u32[]{:S(2)}) copy-start(f32[1024]{0:T(1024)S(1)} %broadcast_multiply_fusion.1) | copy-start | bytes 12292
  10.9 13.7 copy-start.32
  100.1 12.5 copy-start.21
  102.1 10.5 copy-start.25
  119.2 86.1 %copy-start.41 = (s32[1024]{0:T(1024)}, s32[1024]{0:T(1024)S(1)}, u32[]{:S(2)}) copy-start(s32[1024]{0:T(1024)S(1)} %get-tuple-element.248) | copy-start | bytes 12292
  205.2 63.5 %copy-start.13 = (bf16[8,256,768]{2,1,0:T(8,128)(2,1)}, bf16[8,256,768]{2,1,0:T(8,128)(2,1)S(1)}, u32[]{:S(2)}) copy-start(bf16[8,256,768]{2,1,0:T(8,128)(2,1)S(1)} %all_to_all.20) | copy-start | bytes 9437188
  205.2 63.5 %copy-start.44 = (bf16[1,3072,768]{2,1,0:T(8,128)(2,1)S(1)}, bf16[1,3072,768]{2,1,0:T(8,128)(2,1)}, u32[]{:S(2)}) copy-start(bf16[1,3072,768]{2,1,0:T(8,128)(2,1)} %param.37) | copy-start | bytes 14155780
  268.7 11.3 copy-start.51
  280.0 76.2 %all-to-all-start.1 = ((bf16[8,256,768]{2,1,0:T(8,128)(2,1)}), bf16[8,256,768]{2,1,0:T(8,128)(2,1)}, u32[]{:S(2)}, u32[]{:S(2)}) async-start(bf16[8,256,768]{2,1,0:T(8,128)(2,1)} %bitcast.189), calls=%async_computation.1 | async-start | bytes 6291456 | tf_op jit(solution)/shard_map/all_to_all | solution.py:125
  284.7 71.5 %copy-start.38 = (s32[1024]{0:T(1024)S(1)}, s32[1024]{0:T(1024)}, u32[]{:S(2)}) copy-start(s32[1024]{0:T(1024)} %get-tuple-element.247) | copy-start | bytes 12292
  286.4 314.9 %copy-start.8 = (bf16[1024,768]{0,1:T(8,128)(2,1)}, bf16[1024,768]{0,1:T(8,128)(2,1)S(1)}, u32[]{:S(2)}) copy-start(bf16[1024,768]{0,1:T(8,128)(2,1)S(1)} %copy.63) | copy-start | bytes 4718596
  505.4 76.0 %all-to-all-start.3 = ((bf16[8,256,768]{2,1,0:T(8,128)(2,1)}), bf16[8,256,768]{2,1,0:T(8,128)(2,1)}, u32[]{:S(2)}, u32[]{:S(2)}) async-start(bf16[8,256,768]{2,1,0:T(8,128)(2,1)} %bitcast.190), calls=%async_computation.3 | async-start | bytes 6291456 | tf_op jit(solution)/shard_map/all_to_all | solution.py:170
  509.8 462.9 %all-reduce.9.cloned.1.call-start = ((), (), s32[]{:S(2)}) async-start(), calls=%async_computation.4 | async-start | bytes 18874368 | tf_op jit(solution)/shard_map/psum | solution.py:243
  615.6 150.9 %copy-start.2 = (bf16[1024,768]{0,1:T(8,128)(2,1)S(1)}, bf16[1024,768]{0,1:T(8,128)(2,1)}, u32[]{:S(2)}) copy-start(bf16[1024,768]{0,1:T(8,128)(2,1)} %copy-done.1) | copy-start | bytes 4718596
  615.6 150.9 %copy-start.24 = (f32[1024]{0:T(1024)S(1)}, f32[1024]{0:T(1024)}, u32[]{:S(2)}) copy-start(f32[1024]{0:T(1024)} %copy-done.23) | copy-start | bytes 12292
  615.6 150.9 %copy-start.31 = (f32[768]{0:T(1024)S(1)}, f32[768]{0:T(1024)}, u32[]{:S(2)}) copy-start(f32[768]{0:T(1024)} %param.27) | copy-start | bytes 9220
  615.6 151.0 %copy-start.33 = (f32[1024]{0:T(1024)S(1)}, f32[1024]{0:T(1024)}, u32[]{:S(2)}) copy-start(f32[1024]{0:T(1024)} %copy-done.32) | copy-start | bytes 12292
  615.6 151.0 %copy-start.49 = (f32[768]{0:T(1024)S(1)}, f32[768]{0:T(1024)}, u32[]{:S(2)}) copy-start(f32[768]{0:T(1024)} %param.28) | copy-start | bytes 9220
  777.3 389.5 %all-reduce.13.cloned.1.call-start = ((), (), s32[]{:S(2)}) async-start(), calls=%async_computation.6 | async-start | bytes 18874368 | tf_op jit(solution)/shard_map/psum | solution.py:239
  777.3 15.6 %copy-start.14 = (bf16[8,256,768]{2,1,0:T(8,128)(2,1)S(1)}, bf16[8,256,768]{2,1,0:T(8,128)(2,1)}, u32[]{:S(2)}) copy-start(bf16[8,256,768]{2,1,0:T(8,128)(2,1)} %copy-done.13) | copy-start | bytes 9437188
  807.4 553.5 %all-reduce.11.cloned.1.call-start = ((), (), s32[]{:S(2)}) async-start(), calls=%async_computation.5 | async-start | bytes 18874368 | tf_op jit(solution)/shard_map/psum | solution.py:242
  1166.7 7.5 copy-start.12
  (33 other events, 112.7 us)
Sparse Core Ops, SparseCore 0:
  777.4 195.3 all-reduce.8
  977.0 189.6 all-reduce.12
  1170.6 190.2 all-reduce.10
